TPU v7x, 256 devices: a whole 4x4x8 slice. The times are simulated.
256 devices in a mesh: dom: 64 (over y, z, core), rep: 4 (over x).
Axes of the slice: x: 4, y: 4, z: 8, core: 2. Of those that a mesh axis runs over, the one named last changes fastest.
Arguments:
- feats: bfloat16 [256, 262144], P('rep', 'dom'), may hold values from -6 to 6
- w_self: bfloat16 [256, 256], P(None, 'rep'), may hold values from -0.375 to 0.375
- w_neigh: bfloat16 [256, 256], P(None, 'rep'), may hold values from -3 to 3
- local_cols: int32 [2048, 2], P('dom'), may hold values from 0 to 31
- local_tiles: bfloat16 [2048, 2, 128, 128], P('dom'), may hold values from 0 to 3, as said below
- send_list: int32 [64, 64, 2], P('dom'), may hold values from 0 to 31
- remote_rows: int32 [64, 64, 2], P('dom'), may hold values from 0 to 31
- remote_tiles: bfloat16 [64, 64, 2, 128, 128], P('dom'), may hold values from 0 to 3, as said below
- cotangent: bfloat16 [256, 262144], P('rep', 'dom'), may hold values from -6 to 6
Outputs:
- output: bfloat16 [256, 262144], P('rep', 'dom')
- grad_feats: bfloat16 [256, 262144], P('rep', 'dom')
- grad_w_self: float32 [256, 256], P(None, 'rep')
- grad_w_neigh: float32 [256, 256], P(None, 'rep')
Inputs may be any that keep to these rules, and one draw needn't show every extreme that they name: `local_tiles`: edge weights: zero where a tile has no edge, positive otherwise. `remote_tiles`: edge weights: zero where a tile has no edge, positive otherwise.
All inputs are finite; a program needn't handle non-finite values.
Results may differ from a plain program's by a relative error of at most 0.0055.
Values may be sent and summed in bfloat16 or wider, within the bound.
No kernel may reach another device: no remote copies, remote signals or barrier semaphores. Data moves between devices by JAX's collectives and lax.ppermute only.
A program may use at most 128 MiB of HBM per device.

v0:
```python
import jax
import jax.numpy as jnp
from jax import lax
from jax.sharding import PartitionSpec as P


def local(
    feats, w_self, w_neigh, local_cols, local_tiles, send_list, remote_rows, remote_tiles, cotangent
):
    highest = lax.Precision.HIGHEST
    feat_width, node_count = feats.shape
    blocks, local_links, tile_side, _ = local_tiles.shape
    block_ids = jnp.arange(blocks, dtype=jnp.int32)
    blocked = feats.reshape(feat_width, blocks, tile_side)
    outgoing = blocked[:, send_list[0]]
    incoming = lax.all_to_all(outgoing, "dom", split_axis=1, concat_axis=1, tiled=True)
    full_feats = lax.all_gather(feats, "rep", axis=0, tiled=True)
    gathered = blocked[:, local_cols]
    summed = jnp.einsum("fblj,blij->fbi", gathered, local_tiles, preferred_element_type=jnp.float32)
    weight_rows = jnp.sum(local_tiles, axis=(1, 3), dtype=jnp.float32)
    far_tiles = remote_tiles[0]
    far_rows = remote_rows[0]
    placing = (far_rows[:, :, None] == block_ids).astype(jnp.float32)
    far_sums = jnp.sum(far_tiles, axis=3, dtype=jnp.float32)
    divisor = 1.0 + weight_rows + jnp.einsum("ski,skb->bi", far_sums, placing, precision=highest)
    far_terms = jnp.einsum(
        "fskj,skij->fski", incoming, far_tiles, preferred_element_type=jnp.float32
    )
    summed = summed + jnp.einsum("fski,skb->fbi", far_terms, placing, precision=highest)
    aggregate = (summed / divisor).astype(jnp.bfloat16).reshape(feat_width, node_count)
    full_agg = lax.all_gather(aggregate, "rep", axis=0, tiled=True)
    preact = jnp.einsum("ab,an->bn", w_self, full_feats, preferred_element_type=jnp.float32)
    preact = preact + jnp.einsum("ab,an->bn", w_neigh, full_agg, preferred_element_type=jnp.float32)
    sigmoid_val = jax.nn.sigmoid(preact)
    output = (preact * sigmoid_val).astype(jnp.bfloat16)
    slope = sigmoid_val * (1.0 + preact * (1.0 - sigmoid_val))
    grad_pre = (cotangent.astype(jnp.float32) * slope).astype(jnp.bfloat16)
    wg_self = jnp.einsum("an,bn->ab", full_feats, grad_pre, preferred_element_type=jnp.float32)
    wg_neigh = jnp.einsum("an,bn->ab", full_agg, grad_pre, preferred_element_type=jnp.float32)
    wg_self, wg_neigh = lax.psum((wg_self, wg_neigh), "dom")
    term_self = jnp.dot(w_self, grad_pre, preferred_element_type=jnp.float32)
    term_neigh = jnp.dot(w_neigh, grad_pre, preferred_element_type=jnp.float32)
    stacked = lax.psum_scatter(
        jnp.concatenate([term_self, term_neigh], axis=1), "rep", scatter_dimension=0, tiled=True
    )
    back_self = stacked[:, :node_count]
    back_agg = stacked[:, node_count:]
    scaled = (back_agg.reshape(feat_width, blocks, tile_side) / divisor).astype(jnp.bfloat16)
    picked = scaled[:, far_rows]
    far_back = jnp.einsum("fski,skij->fskj", picked, far_tiles, preferred_element_type=jnp.float32)
    returned = lax.all_to_all(far_back, "dom", split_axis=1, concat_axis=1, tiled=True)
    near_back = jnp.einsum(
        "fbi,blij->fblj", scaled, local_tiles, preferred_element_type=jnp.float32
    )
    landing = (local_cols[:, :, None] == block_ids).astype(jnp.float32)
    collected = jnp.einsum("fblj,blc->fcj", near_back, landing, precision=highest)
    homing = (send_list[0][:, :, None] == block_ids).astype(jnp.float32)
    collected = collected + jnp.einsum("fdkj,dkc->fcj", returned, homing, precision=highest)
    grad_feats = (back_self + collected.reshape(feat_width, node_count)).astype(jnp.bfloat16)
    return (output, grad_feats, wg_self, wg_neigh)


def solution(mesh):
    placed = (
        P("rep", "dom"),
        P(None, "rep"),
        P(None, "rep"),
        P("dom", None),
        P("dom", None, None, None),
        P("dom", None, None),
        P("dom", None, None),
        P("dom", None, None, None, None),
        P("rep", "dom"),
    )
    return jax.shard_map(
        local,
        mesh=mesh,
        in_specs=placed,
        out_specs=(P("rep", "dom"), P("rep", "dom"), P(None, "rep"), P(None, "rep")),
        check_vma=False,
    )
```

profile of v0, /device:TPU:1, one launch (start us, length us, event | category | flops | bytes accessed | tf_op | source)
XLA Modules:
  0.0 480.7 jit_solution(3183939513342969295)
XLA Ops:
  7.2 0.0 copy-start
  7.2 0.7 compare_select_fusion.1
  7.9 0.1 copy.42
  8.0 0.1 reshape.94
  8.1 1.2 copy_bitcast_fusion.1
  9.3 2.1 gather_fusion.1
  11.5 13.3 %all-to-all-start = ((bf16[64,64,2,128]{3,0,2,1:T(8,128)(2,1)}), bf16[64,64,2,128]{3,0,2,1:T(8,128)(2,1)S(1)}, u32[]{:S(2)}, u32[]{:S(2)}) async-start(bf16[64,64,2,128]{3,0,2,1:T(8,128)(2,1)} %bitcast.123), calls=%async_computation | async-start | bytes 4194304 | tf_op jit(solution)/shard_map/all_to_all | solution.py:16
  24.8 0.0 all-gather.5.cloned.1.call-start
  24.8 0.1 copy.40
  24.9 0.1 reshape.86
  25.0 1.7 gather_fusion
  26.7 2.2 convert_reduce_fusion.1
  28.9 0.0 copy-start.9
  28.9 3.4 convert_reduce_fusion
  32.3 0.2 fusion.36
  32.5 43.5 %all-to-all-done = bf16[64,64,2,128]{3,0,2,1:T(8,128)(2,1)S(1)} async-done(((bf16[64,64,2,128]{3,0,2,1:T(8,128)(2,1)}), bf16[64,64,2,128]{3,0,2,1:T(8,128)(2,1)S(1)}, u32[]{:S(2)}, u32[]{:S(2)}) %all-to-all-start) | async-done | bytes 2097184 | tf_op jit(solution)/shard_map/all_to_all | solution.py:16
  76.0 5.1 %fusion.8 = f32[64,64,2,128]{3,0,2,1:T(8,128)S(1)} fusion(bf16[64,64,2,128]{3,0,2,1:T(8,128)(2,1)S(1)} %all-to-all-done, bf16[1,64,2,128,128]{4,3,2,1,0:T(8,128)(2,1)} %param.16), kind=kOutput, calls=%fused_computation.18 | convolution fusion | flops 268435456 | bytes 10485760 | tf_op jit(solution)/shard_map/fskj,skij->fski/dot_general | solution.py:26
  81.1 0.0 copy-start.7
  81.2 4.0 fusion.20
  85.2 0.0 copy-done.2
  85.2 0.0 copy-done.7
  85.2 1.1 fusion.35
  86.3 0.0 copy-start.8
  86.3 0.9 copy.87
  87.2 0.0 all-gather.5.cloned.1.call-update
  87.2 0.0 all-gather.3.cloned.1.call-start
  87.2 0.7 all-gather.3.cloned.1.call-update
  87.9 0.2 reduce-scatter.4.cloned.1.call-start
  88.2 29.0 %all-gather.5.cloned.1.call-done = bf16[256,4096]{1,0:T(8,128)(2,1)} async-done(((bf16[64,4096]{1,0:T(8,128)(2,1)}), bf16[256,4096]{1,0:T(8,128)(2,1)}) %all-gather.5.cloned.1.call-update) | async-done | bytes 2097168 | tf_op jit(solution)/shard_map/all_gather | solution.py:31
  117.2 2.1 convolution_bitcast_fusion.2
  119.2 33.2 %all-gather.3.cloned.1.call-done = bf16[256,4096]{1,0:T(8,128)(2,1)} async-done(((bf16[64,4096]{1,0:T(8,128)(2,1)}), bf16[256,4096]{1,0:T(8,128)(2,1)}) %all-gather.3.cloned.1.call-update) | async-done | bytes 2097168 | tf_op jit(solution)/shard_map/all_gather | solution.py:17
  152.4 3.2 multiply_convert_fusion
  155.6 0.7 convolution_bitcast_fusion
  156.3 0.7 convolution_bitcast_fusion.1
  157.1 3.8 pad_maximum_fusion
  160.9 8.9 %copy.60 = f32[256,8192]{1,0:T(8,128)} copy(f32[256,8192]{0,1:T(8,128)} %pad_maximum_fusion) | data formatting | bytes 16777216
  169.8 0.0 reduce-scatter.4.cloned.1.call-update
  169.8 0.1 copy.50
  169.9 0.1 reshape.102
  170.1 83.0 %reduce-scatter.4.cloned.1.call-done = f32[64,8192]{1,0:T(8,128)} async-done(((f32[256,8192]{1,0:T(8,128)}), f32[64,8192]{1,0:T(8,128)}) %reduce-scatter.4.cloned.1.call-update) | async-done | bytes 2097168
  253.1 3.1 fusion.49
  256.2 1.8 copy.63
  258.0 1.6 copy.48
  259.6 1.4 divide_convert_fusion
  261.0 1.0 gather_fusion.2
  261.9 5.4 %fusion.11 = f32[64,64,2,128]{3,0,2,1:T(8,128)} fusion(bf16[64,64,2,128]{3,0,2,1:T(8,128)(2,1)S(1)} %bitcast.121, bf16[1,64,2,128,128]{4,3,2,1,0:T(8,128)(2,1)} %param.16), kind=kOutput, calls=%fused_computation.19 | convolution fusion | flops 268435456 | bytes 10485760 | tf_op jit(solution)/shard_map/fski,skij->fskj/dot_general | solution.py:50
  267.3 11.0 %all-to-all-start.1 = ((f32[64,64,2,128]{3,0,2,1:T(8,128)}), f32[64,64,2,128]{3,0,2,1:T(8,128)}, u32[]{:S(2)}, u32[]{:S(2)}) async-start(f32[64,64,2,128]{3,0,2,1:T(8,128)} %fusion.11), calls=%async_computation.1 | async-start | bytes 8388608 | tf_op jit(solution)/shard_map/all_to_all | solution.py:51
  278.3 0.3 all-reduce.3.cloned.1.call-start
  278.6 1.4 fusion.50
  280.0 0.2 copy-done.6
  280.2 1.4 convolution_bitcast_fusion.5
  281.6 0.0 all-reduce.3.cloned.1.call-update
  281.6 3.4 copy.62
  285.0 0.4 convolution_bitcast_fusion.3
  285.4 0.0 copy-start.11
  285.4 2.1 fusion.17
  287.5 87.6 %all-to-all-done.1 = f32[64,64,2,128]{3,0,2,1:T(8,128)} async-done(((f32[64,64,2,128]{3,0,2,1:T(8,128)}), f32[64,64,2,128]{3,0,2,1:T(8,128)}, u32[]{:S(2)}, u32[]{:S(2)}) %all-to-all-start.1) | async-done | bytes 4194336 | tf_op jit(solution)/shard_map/all_to_all | solution.py:51
  375.1 5.9 %fusion.31 = f32[64,32,128]{2,1,0:T(8,128)S(1)} fusion(f32[32,64,128]{2,0,1:T(8,128)S(1)} %fusion.17, f32[64,64,2,128]{3,0,2,1:T(8,128)} %all-to-all-done.1, s32[64,2]{0,1:T(2,128)S(1)} %bitcast.128), kind=kOutput, calls=%fused_computation.32 | convolution fusion | flops 402919424 | bytes 6291968 | tf_op jit(solution)/shard_map/fdkj,dkc->fcj/dot_general | solution.py:58
  381.0 2.0 copy.59
  383.0 1.8 fusion.14
  384.8 1.1 copy.53
  386.0 85.2 %all-reduce.3.cloned.1.call-done = (f32[256,64]{0,1:T(8,128)}, f32[256,64]{0,1:T(8,128)}) async-done(((f32[256,64]{0,1:T(8,128)}, f32[256,64]{0,1:T(8,128)}), (f32[256,64]{0,1:T(8,128)}, f32[256,64]{0,1:T(8,128)})) %all-reduce.3.cloned.1.call-update) | async-done | bytes 131088 | tf_op jit(solution)/shard_map/psum | solution.py:40
  471.2 1.5 copy.90
  472.7 1.5 copy.91
  (23 shorter events, 0.1 us)
Async XLA Ops:
  7.2 145.3 %copy-start = (bf16[256,64]{0,1:T(8,128)(2,1)S(1)}, bf16[256,64]{0,1:T(8,128)(2,1)}, u32[]{:S(2)}) copy-start(bf16[256,64]{0,1:T(8,128)(2,1)} %param.10) | copy-start | bytes 98308
  11.5 13.3 %copy-start.10 = (s32[32,2]{0,1:T(2,128)S(1)}, s32[32,2]{0,1:T(2,128)}, u32[]{:S(2)}) copy-start(s32[32,2]{0,1:T(2,128)} %param.12) | copy-start | bytes 772
  11.5 64.5 %all-to-all-start = ((bf16[64,64,2,128]{3,0,2,1:T(8,128)(2,1)}), bf16[64,64,2,128]{3,0,2,1:T(8,128)(2,1)S(1)}, u32[]{:S(2)}, u32[]{:S(2)}) async-start(bf16[64,64,2,128]{3,0,2,1:T(8,128)(2,1)} %bitcast.123), calls=%async_computation | async-start | bytes 4194304 | tf_op jit(solution)/shard_map/all_to_all | solution.py:16
  24.8 92.4 %all-gather.5.cloned.1.call-start = ((), (), s32[]{:S(2)}) async-start(), calls=%async_computation.4 | async-start | bytes 2621440 | tf_op jit(solution)/shard_map/all_gather | solution.py:31
  28.9 3.4 copy-start.9
  81.1 4.0 copy-start.2
  81.1 4.0 copy-start.7
  86.3 30.9 %copy-start.8 = (bf16[256,64]{0,1:T(8,128)(2,1)S(1)}, bf16[256,64]{0,1:T(8,128)(2,1)}, u32[]{:S(2)}) copy-start(bf16[256,64]{0,1:T(8,128)(2,1)} %param.11) | copy-start | bytes 98308
  87.2 65.3 %copy-start.12 = (bf16[64,4096]{1,0:T(8,128)(2,1)S(1)}, bf16[64,4096]{1,0:T(8,128)(2,1)}, u32[]{:S(2)}) copy-start(bf16[64,4096]{1,0:T(8,128)(2,1)} %param.17) | copy-start | bytes 1572868
  87.2 65.3 %all-gather.3.cloned.1.call-start = ((), (), s32[]{:S(2)}) async-start(), calls=%async_computation.3 | async-start | bytes 2621440 | tf_op jit(solution)/shard_map/all_gather | solution.py:17
  87.9 165.2 %reduce-scatter.4.cloned.1.call-start = ((), (), s32[]{:S(2)}) async-start(), calls=%async_computation.5 | async-start | bytes 10485760
  267.3 11.2 %copy-start.4 = (bf16[256,4096]{1,0:T(8,128)(2,1)S(1)}, bf16[256,4096]{1,0:T(8,128)(2,1)}, u32[]{:S(2)}) copy-start(bf16[256,4096]{1,0:T(8,128)(2,1)} %all-gather.5.cloned.1.call-done) | copy-start | bytes 6291460
  267.3 107.7 %all-to-all-start.1 = ((f32[64,64,2,128]{3,0,2,1:T(8,128)}), f32[64,64,2,128]{3,0,2,1:T(8,128)}, u32[]{:S(2)}, u32[]{:S(2)}) async-start(f32[64,64,2,128]{3,0,2,1:T(8,128)} %fusion.11), calls=%async_computation.1 | async-start | bytes 8388608 | tf_op jit(solution)/shard_map/all_to_all | solution.py:51
  278.3 192.9 %all-reduce.3.cloned.1.call-start = ((), (), s32[]{:S(2)}) async-start(), calls=%async_computation.6 | async-start | bytes 262144 | tf_op jit(solution)/shard_map/psum | solution.py:40
  278.6 1.6 copy-start.6
  281.6 3.4 copy-start.3
  285.4 89.6 %copy-start.11 = (s32[1,64,2]{1,2,0:T(2,128)S(1)}, s32[1,64,2]{1,2,0:T(2,128)}, u32[]{:S(2)}) copy-start(s32[1,64,2]{1,2,0:T(2,128)} %param.14) | copy-start | bytes 1540
  381.0 2.0 copy-start.5
  383.0 91.1 %copy-start.1 = (bf16[256,64]{0,1:T(8,128)(2,1)S(1)}, bf16[256,64]{0,1:T(8,128)(2,1)}, u32[]{:S(2)}) copy-start(bf16[256,64]{0,1:T(8,128)(2,1)} %param.10) | copy-start | bytes 98308
Sparse Core Ops, SparseCore 0:
  87.3 29.8 all-gather.4
  119.0 33.4 all-gather.2
  169.9 83.1 reduce-scatter.3
  283.0 188.1 all-reduce.2
where the time goes:
time: 482 us; the launch traced here: 481 us
  waiting for transfers between devices  362 us (75%)
  matrix products  33.7 us (7%)
  local copies, waits for them, and re-layouts  32.6 us (7%)
  starting transfers between devices  24.8 us (5%)
  between operations  14 us (3%)
  other arithmetic  13.2 us (3%)
    all_to_all x1, waiting for transfers between devices, local(): lax.all_to_all(far_back, 'dom', split_axis=1, concat_axis=1, tiled=True)  87.6 us
    psum x1, waiting for transfers between devices, local(): wg_self, wg_neigh = lax.psum((wg_self, wg_neigh), 'dom')  85.2 us
    unnamed x5, waiting for transfers between devices  83.8 us
    all_to_all x1, waiting for transfers between devices, local(): lax.all_to_all(outgoing, 'dom', split_axis=1, concat_axis=1, tiled=True)  43.5 us
    all_gather x1, waiting for transfers between devices, local(): full_feats = lax.all_gather(feats, 'rep', axis=0, tiled=True)  33.2 us
    all_gather x1, waiting for transfers between devices, local(): full_agg = lax.all_gather(aggregate, 'rep', axis=0, tiled=True)  29 us
    unnamed x32, local copies, waits for them, and re-layouts  18.5 us
    all_to_all x1, starting transfers between devices, local(): lax.all_to_all(outgoing, 'dom', split_axis=1, concat_axis=1, tiled=True)  13.3 us
  transfers between devices with their start and end apart: 6, of which 6 were waited for; matrix products, arithmetic and copies ran while one was open for 6% of the time, Pallas kernels for 0%

commit v1 on v0

--- a/solution.py
+++ b/solution.py
@@ -2,6 +2,13 @@
 import jax.numpy as jnp
 from jax import lax
 from jax.sharding import PartitionSpec as P
+
+
+def scan_local_data(my_tile, array_axis):
+    upper = list(my_tile.shape[1:])
+    upper[array_axis] *= my_tile.shape[0]
+    piece_next = jnp.moveaxis(my_tile, 0, array_axis).reshape(upper)
+    return piece_next
 
 
 def local(
@@ -28,7 +35,32 @@
     )
     summed = summed + jnp.einsum("fski,skb->fbi", far_terms, placing, precision=highest)
     aggregate = (summed / divisor).astype(jnp.bfloat16).reshape(feat_width, node_count)
-    full_agg = lax.all_gather(aggregate, "rep", axis=0, tiled=True)
+
+    def fix_strips_all(a0, lane_axis, dimension_no):
+        sides = jax.lax.axis_size(lane_axis)
+        slots = []
+        for k in range(sides):
+            slots.append((k, (k + 1) % sides))
+        buffers = []
+        for pp, dev in slots:
+            buffers.append((dev, pp))
+        kept_arr, found_now = ([], [])
+        for idx in range(sides - 1):
+            if idx % 2 == 0:
+                kept_arr.append(
+                    jax.lax.ppermute(kept_arr[-1] if kept_arr else a0, lane_axis, slots)
+                )
+            else:
+                found_now.append(
+                    jax.lax.ppermute(found_now[-1] if found_now else a0, lane_axis, buffers)
+                )
+        z = jnp.stack([*kept_arr[::-1], a0, *found_now], axis=0)
+        w2 = jax.lax.axis_index(lane_axis) - len(kept_arr)
+        z = z[(jnp.arange(sides) - w2) % sides]
+        response = scan_local_data(z, dimension_no)
+        return response
+
+    full_agg = fix_strips_all(aggregate, "rep", 0)
     preact = jnp.einsum("ab,an->bn", w_self, full_feats, preferred_element_type=jnp.float32)
     preact = preact + jnp.einsum("ab,an->bn", w_neigh, full_agg, preferred_element_type=jnp.float32)
     sigmoid_val = jax.nn.sigmoid(preact)

time: 482 us -> 450 us (0.934)
  waiting for transfers between devices: 362 us -> 319 us
  local copies, waits for them, and re-layouts: 32.6 us -> 38.9 us
    all_gather x1, waiting for transfers between devices: 33.2 us -> 0.01 us  [local(): full_feats = lax.all_gather(feats, 'rep', axis=0, tiled=True)]
    all_gather x1 -> x0, waiting for transfers between devices: 29 us -> none  [local(): full_agg = lax.all_gather(aggregate, 'rep', axis=0, tiled=True)]
    ppermute x0 -> x3, waiting for transfers between devices: none -> 24.4 us  [the longest x2 24.4 us: fix_strips_all(): jax.lax.ppermute(kept_arr[-1] if kept_arr else a0, lane_axis, slots)]
    unnamed x5 -> x4, waiting for transfers between devices: 83.8 us -> 80.1 us
    unnamed x32 -> x28, local copies, waits for them, and re-layouts: 18.5 us -> 19.8 us
  transfers between devices with their start and end apart: 6 -> 8, of which waited for: 6 -> 6; matrix products, arithmetic and copies ran while one was open for 6% -> 10% of each run, Pallas kernels for 0% -> 0%
where the time goes in v1:
time: 450 us; the launch traced here: 448 us
  waiting for transfers between devices  319 us (71%)
  local copies, waits for them, and re-layouts  38.9 us (9%)
  matrix products  34.1 us (8%)
  starting transfers between devices  27.2 us (6%)
  other arithmetic  14.9 us (3%)
  between operations  14 us (3%)
    all_to_all x1, waiting for transfers between devices, local(): lax.all_to_all(far_back, 'dom', split_axis=1, concat_axis=1, tiled=True)  87.6 us
    psum x1, waiting for transfers between devices, local(): wg_self, wg_neigh = lax.psum((wg_self, wg_neigh), 'dom')  84.5 us
    unnamed x4, waiting for transfers between devices  80.1 us
    all_to_all x1, waiting for transfers between devices, local(): lax.all_to_all(outgoing, 'dom', split_axis=1, concat_axis=1, tiled=True)  42.8 us
    ppermute x2, waiting for transfers between devices, fix_strips_all(): jax.lax.ppermute(kept_arr[-1] if kept_arr else a0, lane_axis, slots)  24.4 us
    unnamed x28, local copies, waits for them, and re-layouts  19.8 us
    all_to_all x1, starting transfers between devices, local(): lax.all_to_all(outgoing, 'dom', split_axis=1, concat_axis=1, tiled=True)  13.3 us
    all_to_all x1, starting transfers between devices, local(): lax.all_to_all(far_back, 'dom', split_axis=1, concat_axis=1, tiled=True)  10.8 us
  transfers between devices with their start and end apart: 8, of which 6 were waited for; matrix products, arithmetic and copies ran while one was open for 10% of the time, Pallas kernels for 0%

profile of v1, /device:TPU:1, one launch (start us, length us, event | category | flops | bytes accessed | tf_op | source)
XLA Modules:
  0.0 448.5 jit_solution(6771190184848384021)
XLA Ops:
  7.2 0.0 copy-start
  7.2 0.7 compare_select_fusion.1
  7.9 0.1 copy.44
  8.0 0.1 reshape.147
  8.1 1.2 copy_bitcast_fusion.1
  9.3 2.2 gather_fusion.1
  11.5 13.3 %all-to-all-start = ((bf16[64,64,2,128]{3,0,2,1:T(8,128)(2,1)}), bf16[64,64,2,128]{3,0,2,1:T(8,128)(2,1)S(1)}, u32[]{:S(2)}, u32[]{:S(2)}) async-start(bf16[64,64,2,128]{3,0,2,1:T(8,128)(2,1)} %bitcast.129), calls=%async_computation | async-start | bytes 4194304 | tf_op jit(solution)/shard_map/all_to_all | solution.py:23
  24.8 0.0 all-gather.2.cloned.1.call-start
  24.8 0.7 all-gather.2.cloned.1.call-update
  25.5 0.0 reduce-scatter.4.cloned.1.call-start
  25.6 0.1 copy.42
  25.7 0.1 reshape.139
  25.8 1.6 gather_fusion
  27.4 2.2 convert_reduce_fusion.1
  29.6 0.0 copy-start.8
  29.6 3.4 convert_reduce_fusion
  33.1 0.2 fusion.35
  33.3 42.8 %all-to-all-done = bf16[64,64,2,128]{3,0,2,1:T(8,128)(2,1)S(1)} async-done(((bf16[64,64,2,128]{3,0,2,1:T(8,128)(2,1)}), bf16[64,64,2,128]{3,0,2,1:T(8,128)(2,1)S(1)}, u32[]{:S(2)}, u32[]{:S(2)}) %all-to-all-start) | async-done | bytes 2097184 | tf_op jit(solution)/shard_map/all_to_all | solution.py:23
  76.0 5.2 %fusion.8 = f32[64,64,2,128]{3,0,2,1:T(8,128)S(1)} fusion(bf16[64,64,2,128]{3,0,2,1:T(8,128)(2,1)S(1)} %all-to-all-done, bf16[1,64,2,128,128]{4,3,2,1,0:T(8,128)(2,1)} %param.16), kind=kOutput, calls=%fused_computation.19 | convolution fusion | flops 268435456 | bytes 10485760 | tf_op jit(solution)/shard_map/fskj,skij->fski/dot_general | solution.py:33
  81.2 0.0 copy-start.6
  81.2 4.0 fusion.20
  85.2 1.1 fusion.34
  86.3 0.1 copy_bitcast_fusion
  86.3 1.3 collective-permute-start
  87.6 1.5 collective-permute-start.2
  89.1 11.6 %collective-permute-done = bf16[64,4096]{1,0:T(8,128)(2,1)S(1)} collective-permute-done((bf16[64,4096]{1,0:T(8,128)(2,1)S(1)}, bf16[64,4096]{1,0:T(8,128)(2,1)S(1)}, u32[]{:S(2)}, u32[]{:S(2)}) %collective-permute-start) | collective-permute-done | bytes 524320 | tf_op jit(solution)/shard_map/ppermute | solution.py:51
  100.8 0.3 copy.49
  101.1 0.2 stack_reshape.3
  101.4 12.8 %collective-permute-done.1 = bf16[64,4096]{1,0:T(8,128)(2,1)S(1)} collective-permute-done((bf16[64,4096]{1,0:T(8,128)(2,1)S(1)}, bf16[64,4096]{1,0:T(8,128)(2,1)S(1)}, u32[]{:S(2)}, u32[]{:S(2)}) %collective-permute-start.1) | collective-permute-done | bytes 524320 | tf_op jit(solution)/shard_map/ppermute | solution.py:51
  114.1 1.6 pad_maximum_fusion.1
  115.7 2.3 gather_fusion.2
  118.0 1.5 convolution_bitcast_fusion.2
  119.5 3.6 multiply_convert_fusion
  123.1 0.7 convolution_bitcast_fusion
  123.8 0.7 convolution_bitcast_fusion.1
  124.6 3.8 pad_maximum_fusion
  128.4 9.0 %copy.63 = f32[256,8192]{1,0:T(8,128)} copy(f32[256,8192]{0,1:T(8,128)} %pad_maximum_fusion) | data formatting | bytes 16777216
  137.3 0.0 reduce-scatter.4.cloned.1.call-update
  137.4 0.1 copy.53
  137.5 0.1 reshape.163
  137.6 79.4 %reduce-scatter.4.cloned.1.call-done = f32[64,8192]{1,0:T(8,128)} async-done(((f32[256,8192]{1,0:T(8,128)}), f32[64,8192]{1,0:T(8,128)}) %reduce-scatter.4.cloned.1.call-update) | async-done | bytes 2097168
  217.0 3.1 fusion.50
  220.1 3.2 copy.66
  223.3 3.2 copy.51
  226.5 1.4 divide_convert_fusion
  227.8 2.2 gather_fusion.3
  230.0 6.0 %fusion.11 = f32[64,64,2,128]{3,0,2,1:T(8,128)} fusion(bf16[64,64,2,128]{3,0,2,1:T(8,128)(2,1)} %bitcast.127, bf16[1,64,2,128,128]{4,3,2,1,0:T(8,128)(2,1)} %param.16), kind=kOutput, calls=%fused_computation.20 | convolution fusion | flops 268435456 | bytes 10485760 | tf_op jit(solution)/shard_map/fski,skij->fskj/dot_general | solution.py:82
  236.0 10.8 %all-to-all-start.1 = ((f32[64,64,2,128]{3,0,2,1:T(8,128)}), f32[64,64,2,128]{3,0,2,1:T(8,128)}, u32[]{:S(2)}, u32[]{:S(2)}) async-start(f32[64,64,2,128]{3,0,2,1:T(8,128)} %fusion.11), calls=%async_computation.1 | async-start | bytes 8388608 | tf_op jit(solution)/shard_map/all_to_all | solution.py:83
  246.8 0.3 all-reduce.3.cloned.1.call-start
  247.1 1.4 fusion.51
  248.5 0.2 copy-done.5
  248.7 1.4 convolution_bitcast_fusion.5
  250.1 0.0 all-reduce.3.cloned.1.call-update
  250.1 3.4 copy.65
  253.5 0.4 convolution_bitcast_fusion.3
  254.0 2.1 fusion.17
  256.0 87.6 %all-to-all-done.1 = f32[64,64,2,128]{3,0,2,1:T(8,128)} async-done(((f32[64,64,2,128]{3,0,2,1:T(8,128)}), f32[64,64,2,128]{3,0,2,1:T(8,128)}, u32[]{:S(2)}, u32[]{:S(2)}) %all-to-all-start.1) | async-done | bytes 4194336 | tf_op jit(solution)/shard_map/all_to_all | solution.py:83
  343.6 5.9 %fusion.31 = f32[64,32,128]{2,1,0:T(8,128)S(1)} fusion(f32[32,64,128]{2,0,1:T(8,128)S(1)} %fusion.17, f32[64,64,2,128]{3,0,2,1:T(8,128)} %all-to-all-done.1, s32[64,2]{0,1:T(2,128)S(1)} %bitcast.137), kind=kOutput, calls=%fused_computation.34 | convolution fusion | flops 402919424 | bytes 6291968 | tf_op jit(solution)/shard_map/fdkj,dkc->fcj/dot_general | solution.py:90
  349.5 2.0 copy.62
  351.6 1.8 fusion.14
  353.4 1.1 copy.56
  354.5 84.5 %all-reduce.3.cloned.1.call-done = (f32[256,64]{0,1:T(8,128)}, f32[256,64]{0,1:T(8,128)}) async-done(((f32[256,64]{0,1:T(8,128)}, f32[256,64]{0,1:T(8,128)}), (f32[256,64]{0,1:T(8,128)}, f32[256,64]{0,1:T(8,128)})) %all-reduce.3.cloned.1.call-update) | async-done | bytes 131088 | tf_op jit(solution)/shard_map/psum | solution.py:72
  439.0 1.5 copy.92
  440.5 1.5 copy.93
  (28 shorter events, 0.1 us)
Async XLA Ops:
  7.2 112.3 %copy-start = (bf16[256,64]{0,1:T(8,128)(2,1)S(1)}, bf16[256,64]{0,1:T(8,128)(2,1)}, u32[]{:S(2)}) copy-start(bf16[256,64]{0,1:T(8,128)(2,1)} %param.10) | copy-start | bytes 98308
  11.5 14.1 %copy-start.9 = (s32[32,2]{0,1:T(2,128)S(1)}, s32[32,2]{0,1:T(2,128)}, u32[]{:S(2)}) copy-start(s32[32,2]{0,1:T(2,128)} %param.12) | copy-start | bytes 772
  11.5 64.5 %all-to-all-start = ((bf16[64,64,2,128]{3,0,2,1:T(8,128)(2,1)}), bf16[64,64,2,128]{3,0,2,1:T(8,128)(2,1)S(1)}, u32[]{:S(2)}, u32[]{:S(2)}) async-start(bf16[64,64,2,128]{3,0,2,1:T(8,128)(2,1)} %bitcast.129), calls=%async_computation | async-start | bytes 4194304 | tf_op jit(solution)/shard_map/all_to_all | solution.py:23
  24.8 94.7 %all-gather.2.cloned.1.call-start = ((), (), s32[]{:S(2)}) async-start(), calls=%async_computation.3 | async-start | bytes 2621440 | tf_op jit(solution)/shard_map/all_gather | solution.py:24
  25.5 191.5 %reduce-scatter.4.cloned.1.call-start = ((), (), s32[]{:S(2)}) async-start(), calls=%async_computation.4 | async-start | bytes 10485760
  29.6 3.4 copy-start.8
  81.2 4.0 copy-start.2
  81.2 4.0 copy-start.6
  86.3 14.4 %collective-permute-start = (bf16[64,4096]{1,0:T(8,128)(2,1)S(1)}, bf16[64,4096]{1,0:T(8,128)(2,1)S(1)}, u32[]{:S(2)}, u32[]{:S(2)}) collective-permute-start(bf16[64,4096]{1,0:T(8,128)(2,1)S(1)} %copy_bitcast_fusion), channel_id=1, source_target_pairs={{0,1},{1,2},{2,3},{3,0},{4,5},{5,6},{6,7},{7,4},{8,9},{9,10},{10,1... | collective-permute-start | bytes 1572872 | tf_op jit(solution)/shard_map/ppermute | solution.py:51
  87.6 13.7 %collective-permute-start.2 = (bf16[64,4096]{1,0:T(8,128)(2,1)S(1)}, bf16[64,4096]{1,0:T(8,128)(2,1)S(1)}, u32[]{:S(2)}, u32[]{:S(2)}) collective-permute-start(bf16[64,4096]{1,0:T(8,128)(2,1)S(1)} %copy_bitcast_fusion), channel_id=1, source_target_pairs={{1,0},{2,1},{3,2},{0,3},{5,4},{6,5},{7,6},{4,7},{9,8},{10,9},{11,1... | collective-permute-start | bytes 1572872 | tf_op jit(solution)/shard_map/ppermute | solution.py:55
  100.7 13.4 %collective-permute-start.1 = (bf16[64,4096]{1,0:T(8,128)(2,1)S(1)}, bf16[64,4096]{1,0:T(8,128)(2,1)S(1)}, u32[]{:S(2)}, u32[]{:S(2)}) collective-permute-start(bf16[64,4096]{1,0:T(8,128)(2,1)S(1)} %collective-permute-done), channel_id=1, source_target_pairs={{0,1},{1,2},{2,3},{3,0},{4,5},{5,6},{6,7},{7,4},{8,9},{9,10},{10,1... | collective-permute-start | bytes 1572872 | tf_op jit(solution)/shard_map/ppermute | solution.py:51
  115.7 2.3 copy-start.7
  236.0 107.6 %all-to-all-start.1 = ((f32[64,64,2,128]{3,0,2,1:T(8,128)}), f32[64,64,2,128]{3,0,2,1:T(8,128)}, u32[]{:S(2)}, u32[]{:S(2)}) async-start(f32[64,64,2,128]{3,0,2,1:T(8,128)} %fusion.11), calls=%async_computation.1 | async-start | bytes 8388608 | tf_op jit(solution)/shard_map/all_to_all | solution.py:83
  246.8 192.2 %all-reduce.3.cloned.1.call-start = ((), (), s32[]{:S(2)}) async-start(), calls=%async_computation.5 | async-start | bytes 262144 | tf_op jit(solution)/shard_map/psum | solution.py:72
  247.1 1.6 copy-start.5
  250.1 3.4 copy-start.3
  253.9 89.7 %copy-start.10 = (s32[1,64,2]{1,2,0:T(2,128)S(1)}, s32[1,64,2]{1,2,0:T(2,128)}, u32[]{:S(2)}) copy-start(s32[1,64,2]{1,2,0:T(2,128)} %param.14) | copy-start | bytes 1540
  349.5 2.1 copy-start.4
  351.6 90.4 %copy-start.1 = (bf16[256,64]{0,1:T(8,128)(2,1)S(1)}, bf16[256,64]{0,1:T(8,128)(2,1)}, u32[]{:S(2)}) copy-start(bf16[256,64]{0,1:T(8,128)(2,1)} %param.10) | copy-start | bytes 98308
Sparse Core Ops, SparseCore 0:
  27.4 34.3 all-gather.1
  137.5 79.4 reduce-scatter.3
  251.8 187.1 all-reduce.2
